TPU v7x, 32 devices: a whole 2x2x4 slice. The times are simulated.
32 devices in a mesh: sec: 4 (over y, x), term: 8 (over z, core).
Axes of the slice: x: 2, y: 2, z: 4, core: 2. Of those that a mesh axis runs over, the one named last changes fastest.
Arguments:
- theta: bfloat16 [4, 896, 896], P('sec', 'term'), may hold values from -6 to 6
- left_env: bfloat16 [16, 4, 896, 896], P('term', 'sec'), may hold values from -2 to 2
- right_env: bfloat16 [16, 4, 896, 896], P('term', 'sec'), may hold values from -2 to 2
- term_shift: int32 [16], P('term'), may hold values from -1 to 1
- term_on: int32 [16, 4], P('term', 'sec'), may hold values 0 or 1
- block_rows: int32 [4], P('sec'), may hold values from 224 to 896
- block_cols: int32 [4], P('sec'), may hold values from 224 to 896
Outputs:
- basis_last: float32 [4, 896, 896], P('sec', 'term')
- alphas: float32 [2], replicated
- betas: float32 [2], replicated
All inputs are finite; a program needn't handle non-finite values. No bound on the sum of `term_on` on one device may be relied on, other than what follows from the above.
Results may differ from a plain program's by a relative error of at most 0.0037.
Values may be sent and summed in bfloat16 or wider, within the bound.
No kernel may reach another device: no remote copies, remote signals or barrier semaphores. Data moves between devices by JAX's collectives and lax.ppermute only.
A program may use at most 64 MiB of HBM per device.

v0:
```python
import jax
import jax.numpy as jnp
from jax import lax
from jax.sharding import PartitionSpec as P

ITERS = 2
EPS = 1e-06


def extended(block, sides, width):
    for axis, dim in sides:
        count = lax.axis_size(axis)
        forward = [(i, i + 1) for i in range(count - 1)]
        backward = [(target, source) for source, target in forward]
        low = lax.ppermute(
            lax.slice_in_dim(block, block.shape[dim] - width, None, axis=dim), axis, forward
        )
        high = lax.ppermute(lax.slice_in_dim(block, 0, width, axis=dim), axis, backward)
        block = jnp.concatenate([low, block, high], axis=dim)
    return block


def on_device(theta, left_env, right_env, term_shift, term_on, block_rows, block_cols):
    sectors = theta.shape[0]
    row_count = theta.shape[1]
    width = theta.shape[2]
    terms_here = left_env.shape[0]
    full_count = row_count * lax.axis_size("term")
    row_offset = lax.axis_index("term") * row_count
    col_line = jnp.arange(width, dtype=jnp.int32)
    col_mask = (col_line[None, :] < block_cols[:, None]).astype(jnp.float32)
    local_rows = row_offset + jnp.arange(row_count, dtype=jnp.int32)
    row_mask = (local_rows[None, :] < block_rows[:, None]).astype(jnp.float32)
    mask = row_mask[:, :, None] * col_mask[:, None, :]
    on_float = term_on.astype(jnp.float32)
    start = mask * theta.astype(jnp.float32)
    norm_start = lax.psum(jnp.sum(start * start), ("sec", "term"))
    vector = start / jnp.sqrt(norm_start + EPS)
    previous = jnp.zeros_like(vector)
    beta_prev = jnp.float32(0.0)
    alpha_list = []
    beta_list = []
    for step in range(ITERS):
        vector_bf = vector.astype(jnp.bfloat16)
        full_rows = lax.all_gather(vector_bf, "term", axis=1, tiled=True)
        padded = extended(full_rows, (("sec", 0),), 1)
        source_list = [
            lax.dynamic_slice_in_dim(padded, 1 + term_shift[term_index], sectors, 0)
            for term_index in range(terms_here)
        ]
        total = jnp.zeros((full_count, sectors, width), jnp.float32)
        for partial_term_index in range(terms_here):
            left_rows = left_env[partial_term_index]
            product = jnp.einsum(
                "sik,skj->sij",
                left_rows,
                source_list[partial_term_index],
                preferred_element_type=jnp.float32,
            ).astype(jnp.bfloat16)
            result = jnp.einsum(
                "sij,sjk->isk",
                product,
                right_env[partial_term_index],
                preferred_element_type=jnp.float32,
            )
            total = total + on_float[partial_term_index][None, :, None] * result
        row_index = jnp.arange(full_count, dtype=jnp.int32)
        rows_inside = (row_index[:, None] < block_rows[None, :]).astype(jnp.float32)
        total = total * rows_inside[:, :, None] * col_mask[None, :, :]
        summed = lax.psum(total.reshape(full_count, sectors * width), "term")
        scattered = lax.dynamic_slice_in_dim(summed, row_offset, row_count, 0)
        image = scattered.reshape(row_count, sectors, width).transpose(1, 0, 2)
        alpha = lax.psum(jnp.sum(vector * image), ("sec", "term"))
        residual = image - alpha * vector - beta_prev * previous
        beta_square = lax.psum(jnp.sum(residual * residual), ("sec", "term"))
        beta = jnp.sqrt(beta_square + EPS)
        previous = vector
        vector = residual / beta
        beta_prev = beta
        alpha_list.append(alpha)
        beta_list.append(beta)
    return (vector, jnp.stack(alpha_list), jnp.stack(beta_list))


def solution(mesh):
    return jax.shard_map(
        on_device,
        mesh=mesh,
        in_specs=(
            P("sec", "term", None),
            P("term", "sec", None, None),
            P("term", "sec", None, None),
            P("term"),
            P("term", "sec"),
            P("sec"),
            P("sec"),
        ),
        out_specs=(P("sec", "term", None), P(), P()),
        check_vma=False,
    )
```

profile of v0, /device:TPU:0, one launch (start us, length us, event | category | flops | bytes accessed | tf_op | source)
XLA Modules:
  0.0 632.7 jit_solution(16715820950023222964)
XLA Ops:
  8.5 1.7 multiply_reduce_fusion.2
  10.2 42.2 %psum.49 = f32[]{:T(128)} all-reduce(f32[]{:T(128)} %multiply_reduce_fusion.2), channel_id=1, replica_groups=mesh['sec'=4,'term'=8] {'sec','term'}, use_global_device_ids=true, to_apply=%region_1.0 | all-reduce | flops 1 | bytes 8 | tf_op jit(solution)/shard_map/psum | solution.py:37
  53.1 1.7 fusion.61
  55.0 25.3 %all-gather.3.cloned.1.call-done = bf16[1,896,896]{2,1,0:T(8,128)(2,1)} async-done(((bf16[1,112,896]{2,1,0:T(8,128)(2,1)}), bf16[1,896,896]{2,1,0:T(8,128)(2,1)}) %all-gather.3.cloned.1.call-update) | async-done | bytes 1605648 | tf_op jit(solution)/shard_map/all_gather | solution.py:45
  80.3 4.7 collective-permute-start
  86.2 1.3 fusion.63
  91.4 27.4 %collective-permute-done = bf16[1,896,896]{2,1,0:T(8,128)(2,1)} collective-permute-done((bf16[1,896,896]{2,1,0:T(8,128)(2,1)}, bf16[1,896,896]{2,1,0:T(8,128)(2,1)}, u32[]{:S(2)}, u32[]{:S(2)}) %collective-permute-start) | collective-permute-done | bytes 1605664 | tf_op jit(solution)/shard_map/ppermute | solution.py:15
  118.8 2.7 constant_dynamic-update-slice_fusion.2
  122.9 32.2 %collective-permute-done.1 = bf16[1,896,896]{2,1,0:T(8,128)(2,1)S(1)} collective-permute-done((bf16[1,896,896]{2,1,0:T(8,128)(2,1)}, bf16[1,896,896]{2,1,0:T(8,128)(2,1)S(1)}, u32[]{:S(2)}, u32[]{:S(2)}) %collective-permute-start.1) | collective-permute-done | bytes 1605664 | tf_op jit(solution)/shard_map/ppermute | solution.py:18
  155.1 1.3 constant_dynamic-update-slice_fusion
  156.4 8.2 %fusion.13 = f32[896,896]{1,0:T(8,128)} fusion(bf16[2,1,896,896]{3,2,1,0:T(8,128)(2,1)} %param.9, bf16[3,896,896]{2,1,0:T(8,128)(2,1)} %constant_dynamic-update-slice_fusion, s32[]{:T(128)S(6)} %select_n.12, bf16[2,1,896,896]{3,2,1,0:T(8,128)(2,1)} %param.8), kind=kOutput, calls=%fused_computation.19 | convolution fusion | flops 2878095360 | bytes 8028164 | tf_op jit(solution)/shard_map/sij,sjk->isk/dot_general | solution.py:60
  164.6 10.1 %fusion.3 = f32[896,896]{1,0:T(8,128)} fusion(f32[896,896]{1,0:T(8,128)} %fusion.13, f32[896]{0:T(1024)S(1)} %fusion.50, f32[896]{0:T(1024)S(1)} %fusion.51, f32[]{:T(128)} %bitcast.8, f32[]{:T(128)} %bitcast, bf16[2,1,896,896]{3,2,1,0:T(8,128)(2,1)S(1)} %copy-done.3, bf16[3,896,896]{2,1,0:T(8,128)(2,1)} %constant_dynamic-update-slice_fusion, ...), kind=kOutput, calls=%fused_computation.5 | convolution fusion | flops 2882109440 | bytes 11248644 | tf_op jit(solution)/shard_map/sij,sjk->isk/dot_general | solution.py:60
  174.8 76.8 %all-reduce.3.cloned.1.call-done = f32[896,896]{1,0:T(8,128)} async-done(((f32[896,896]{1,0:T(8,128)}), f32[896,896]{1,0:T(8,128)}) %all-reduce.3.cloned.1.call-update) | async-done | bytes 3211280 | tf_op jit(solution)/shard_map/psum | solution.py:70
  251.5 1.8 fusion.48
  253.3 40.4 %psum.51 = f32[]{:T(128)} all-reduce(f32[]{:T(128)} %fusion.48), channel_id=1, replica_groups=mesh['sec'=4,'term'=8] {'sec','term'}, use_global_device_ids=true, to_apply=%region_4.0 | all-reduce | flops 1 | bytes 8 | tf_op jit(solution)/shard_map/psum | solution.py:73
  293.7 2.4 multiply_reduce_fusion.1
  296.1 39.6 %psum.52 = f32[]{:T(128)} all-reduce(f32[]{:T(128)} %multiply_reduce_fusion.1), channel_id=1, replica_groups=mesh['sec'=4,'term'=8] {'sec','term'}, use_global_device_ids=true, to_apply=%region_6.0 | all-reduce | flops 1 | bytes 8 | tf_op jit(solution)/shard_map/psum | solution.py:75
  336.4 2.5 fusion.60
  339.1 26.1 %all-gather.5.cloned.1.call-done = bf16[1,896,896]{2,1,0:T(8,128)(2,1)} async-done(((bf16[1,112,896]{2,1,0:T(8,128)(2,1)}), bf16[1,896,896]{2,1,0:T(8,128)(2,1)}) %all-gather.5.cloned.1.call-update) | async-done | bytes 1605648 | tf_op jit(solution)/shard_map/all_gather | solution.py:45
  365.2 3.6 collective-permute-start.2
  370.1 33.6 %collective-permute-done.2 = bf16[1,896,896]{2,1,0:T(8,128)(2,1)S(1)} collective-permute-done((bf16[1,896,896]{2,1,0:T(8,128)(2,1)}, bf16[1,896,896]{2,1,0:T(8,128)(2,1)S(1)}, u32[]{:S(2)}, u32[]{:S(2)}) %collective-permute-start.2) | collective-permute-done | bytes 1605664 | tf_op jit(solution)/shard_map/ppermute | solution.py:15
  403.7 1.3 constant_dynamic-update-slice_fusion.5
  406.3 33.6 %collective-permute-done.3 = bf16[1,896,896]{2,1,0:T(8,128)(2,1)S(1)} collective-permute-done((bf16[1,896,896]{2,1,0:T(8,128)(2,1)}, bf16[1,896,896]{2,1,0:T(8,128)(2,1)S(1)}, u32[]{:S(2)}, u32[]{:S(2)}) %collective-permute-start.3) | collective-permute-done | bytes 1605664 | tf_op jit(solution)/shard_map/ppermute | solution.py:18
  439.9 1.3 constant_dynamic-update-slice_fusion.3
  441.2 8.1 %fusion.11 = f32[896,896]{1,0:T(8,128)} fusion(bf16[2,1,896,896]{3,2,1,0:T(8,128)(2,1)} %param.9, bf16[3,896,896]{2,1,0:T(8,128)(2,1)} %constant_dynamic-update-slice_fusion.3, s32[]{:T(128)S(6)} %select_n.12, bf16[2,1,896,896]{3,2,1,0:T(8,128)(2,1)} %param.8), kind=kOutput, calls=%fused_computation.17 | convolution fusion | flops 2878095360 | bytes 8028164 | tf_op jit(solution)/shard_map/sij,sjk->isk/dot_general | solution.py:60
  449.3 10.6 %fusion.1 = f32[896,896]{1,0:T(8,128)} fusion(f32[896,896]{1,0:T(8,128)} %fusion.11, f32[896]{0:T(1024)S(1)} %fusion.50, f32[896]{0:T(1024)S(1)} %fusion.51, f32[]{:T(128)} %bitcast.8, f32[]{:T(128)} %bitcast, bf16[2,1,896,896]{3,2,1,0:T(8,128)(2,1)} %param.9, bf16[3,896,896]{2,1,0:T(8,128)(2,1)} %constant_dynamic-update-slice_fusion.3, s32[]{:T(128)S(6)} %select_n.13, ...), kind=kOutput, calls=%fused_computation.2 | convolution fusion | flops 2882109440 | bytes 11247620 | tf_op jit(solution)/shard_map/sij,sjk->isk/dot_general | solution.py:60
  459.9 76.8 %all-reduce.5.cloned.1.call-done = f32[896,896]{1,0:T(8,128)} async-done(((f32[896,896]{1,0:T(8,128)}), f32[896,896]{1,0:T(8,128)}) %all-reduce.5.cloned.1.call-update) | async-done | bytes 3211280 | tf_op jit(solution)/shard_map/psum | solution.py:70
  536.7 2.5 fusion.46
  539.2 40.4 %psum.54 = f32[]{:T(128)} all-reduce(f32[]{:T(128)} %fusion.46), channel_id=1, replica_groups=mesh['sec'=4,'term'=8] {'sec','term'}, use_global_device_ids=true, to_apply=%region_9.0 | all-reduce | flops 1 | bytes 8 | tf_op jit(solution)/shard_map/psum | solution.py:73
  579.6 3.2 multiply_reduce_fusion
  582.8 39.5 %psum.55 = f32[]{:T(128)} all-reduce(f32[]{:T(128)} %get-tuple-element.3), channel_id=1, replica_groups=mesh['sec'=4,'term'=8] {'sec','term'}, use_global_device_ids=true, to_apply=%region_11.0 | all-reduce | flops 1 | bytes 8 | tf_op jit(solution)/shard_map/psum | solution.py:75
  624.4 1.7 pad_maximum_fusion
  (27 shorter events, 8.2 us)
Async XLA Ops:
  7.2 73.1 %all-gather.3.cloned.1.call-start = ((), (), s32[]{:S(2)}) async-start(), calls=%async_computation | async-start | bytes 1806336 | tf_op jit(solution)/shard_map/all_gather | solution.py:45
  54.9 196.6 %all-reduce.3.cloned.1.call-start = ((), (), s32[]{:S(2)}) async-start(), calls=%async_computation.1 | async-start | bytes 6422528 | tf_op jit(solution)/shard_map/psum | solution.py:70
  80.3 41.3 %copy-start.1 = (bf16[1,896,896]{2,1,0:T(8,128)(2,1)S(1)}, bf16[1,896,896]{2,1,0:T(8,128)(2,1)}, u32[]{:S(2)}) copy-start(bf16[1,896,896]{2,1,0:T(8,128)(2,1)} %all-gather.3.cloned.1.call-done) | copy-start | bytes 4816900
  80.3 38.6 %collective-permute-start = (bf16[1,896,896]{2,1,0:T(8,128)(2,1)}, bf16[1,896,896]{2,1,0:T(8,128)(2,1)}, u32[]{:S(2)}, u32[]{:S(2)}) collective-permute-start(bf16[1,896,896]{2,1,0:T(8,128)(2,1)} %all-gather.3.cloned.1.call-done), channel_id=1, source_target_pairs={{0,8},{8,16},{16,24},{1,9},{9,17},{17,25},{2,10},{10,18},{18,26},{... | collective-permute-start | bytes 4816904 | tf_op jit(solution)/shard_map/ppermute | solution.py:15
  85.0 70.1 %collective-permute-start.1 = (bf16[1,896,896]{2,1,0:T(8,128)(2,1)}, bf16[1,896,896]{2,1,0:T(8,128)(2,1)S(1)}, u32[]{:S(2)}, u32[]{:S(2)}) collective-permute-start(bf16[1,896,896]{2,1,0:T(8,128)(2,1)} %all-gather.3.cloned.1.call-done), channel_id=1, source_target_pairs={{8,0},{16,8},{24,16},{9,1},{17,9},{25,17},{10,2},{18,10},{26,18},{... | collective-permute-start | bytes 4816904 | tf_op jit(solution)/shard_map/ppermute | solution.py:18
  156.4 8.2 %copy-start.3 = (bf16[2,1,896,896]{3,2,1,0:T(8,128)(2,1)S(1)}, bf16[2,1,896,896]{3,2,1,0:T(8,128)(2,1)}, u32[]{:S(2)}) copy-start(bf16[2,1,896,896]{3,2,1,0:T(8,128)(2,1)} %param.9) | copy-start | bytes 9633796
  174.7 76.8 %copy-start = (bf16[1,112,896]{2,1,0:T(8,128)(2,1)S(1)}, bf16[1,112,896]{2,1,0:T(8,128)(2,1)}, u32[]{:S(2)}) copy-start(bf16[1,112,896]{2,1,0:T(8,128)(2,1)} %param.7) | copy-start | bytes 602116
  174.7 190.4 %all-gather.5.cloned.1.call-start = ((), (), s32[]{:S(2)}) async-start(), calls=%async_computation.2 | async-start | bytes 1806336 | tf_op jit(solution)/shard_map/all_gather | solution.py:45
  338.9 197.9 %all-reduce.5.cloned.1.call-start = ((), (), s32[]{:S(2)}) async-start(), calls=%async_computation.3 | async-start | bytes 6422528 | tf_op jit(solution)/shard_map/psum | solution.py:70
  365.2 39.9 %copy-start.2 = (bf16[1,896,896]{2,1,0:T(8,128)(2,1)S(1)}, bf16[1,896,896]{2,1,0:T(8,128)(2,1)}, u32[]{:S(2)}) copy-start(bf16[1,896,896]{2,1,0:T(8,128)(2,1)} %all-gather.5.cloned.1.call-done) | copy-start | bytes 4816900
  365.2 38.5 %collective-permute-start.2 = (bf16[1,896,896]{2,1,0:T(8,128)(2,1)}, bf16[1,896,896]{2,1,0:T(8,128)(2,1)S(1)}, u32[]{:S(2)}, u32[]{:S(2)}) collective-permute-start(bf16[1,896,896]{2,1,0:T(8,128)(2,1)} %all-gather.5.cloned.1.call-done), channel_id=1, source_target_pairs={{0,8},{8,16},{16,24},{1,9},{9,17},{17,25},{2,10},{10,18},{18,26},{... | collective-permute-start | bytes 4816904 | tf_op jit(solution)/shard_map/ppermute | solution.py:15
  368.8 71.2 %collective-permute-start.3 = (bf16[1,896,896]{2,1,0:T(8,128)(2,1)}, bf16[1,896,896]{2,1,0:T(8,128)(2,1)S(1)}, u32[]{:S(2)}, u32[]{:S(2)}) collective-permute-start(bf16[1,896,896]{2,1,0:T(8,128)(2,1)} %all-gather.5.cloned.1.call-done), channel_id=1, source_target_pairs={{8,0},{16,8},{24,16},{9,1},{17,9},{25,17},{10,2},{18,10},{26,18},{... | collective-permute-start | bytes 4816904 | tf_op jit(solution)/shard_map/ppermute | solution.py:18
Sparse Core Ops, SparseCore 0:
  55.0 25.2 all-gather.2
  174.8 76.6 all-reduce.2
  339.0 26.1 all-gather.4
  460.0 76.6 all-reduce.4
where the time goes:
time: 634 us; the launch traced here: 633 us
  waiting for transfers between devices  332 us (52%)
  blocking collectives  202 us (32%)
  matrix products  36.9 us (6%)
  between operations  19.8 us (3%)
  other arithmetic  19.6 us (3%)
  starting transfers between devices  11.2 us (2%)
  local copies, waits for them, and re-layouts  11.1 us (2%)
    psum x2, waiting for transfers between devices, on_device(): summed = lax.psum(total.reshape(full_count, sectors * width), 'term')  154 us
    psum x2, blocking collectives, on_device(): alpha = lax.psum(jnp.sum(vector * image), ('sec', 'term'))  80.8 us
    psum x2, blocking collectives, on_device(): beta_square = lax.psum(jnp.sum(residual * residual), ('sec', 'term'))  79.1 us
    ppermute x2, waiting for transfers between devices, extended(): lax.ppermute(lax.slice_in_dim(block, 0, width, axis=dim), axis, backward)  65.8 us
    ppermute x2, waiting for transfers between devices, extended(): lax.ppermute(lax.slice_in_dim(block, block.shape[dim] - width, None, axis...  61.1 us
    all_gather x2, waiting for transfers between devices, on_device(): full_rows = lax.all_gather(vector_bf, 'term', axis=1, tiled=True)  51.4 us
    psum x1, blocking collectives, on_device(): norm_start = lax.psum(jnp.sum(start * start), ('sec', 'term'))  42.2 us
    dot_general x4, matrix products, on_device(): jnp.einsum('sij,sjk->isk', product, right_env[partial_term_index], prefer...  36.9 us
  transfers between devices with their start and end apart: 8, of which 8 were waited for; matrix products, arithmetic and copies ran while one was open for 1% of the time, Pallas kernels for 0%

commit v1 on v0

--- a/solution.py
+++ b/solution.py
@@ -42,7 +42,14 @@
     beta_list = []
     for step in range(ITERS):
         vector_bf = vector.astype(jnp.bfloat16)
-        full_rows = lax.all_gather(vector_bf, "term", axis=1, tiled=True)
+        ring = [vector_bf]
+        for hop in range(7):
+            ring.append(lax.ppermute(ring[-1], "term", [(dev, (dev + 1) % 8) for dev in range(8)]))
+        full_rows = jnp.roll(
+            jnp.concatenate(ring[::-1], axis=1),
+            (lax.axis_index("term") + 1) * ring[0].shape[1],
+            axis=1,
+        )
         padded = extended(full_rows, (("sec", 0),), 1)
         source_list = [
             lax.dynamic_slice_in_dim(padded, 1 + term_shift[term_index], sectors, 0)

time: 634 us -> 674 us (1.063)
  waiting for transfers between devices: 332 us -> 370 us
  other arithmetic: 19.6 us -> 29.6 us
  local copies, waits for them, and re-layouts: 11.1 us -> 1.55 us
    ppermute x0 -> x14, waiting for transfers between devices: none -> 97.1 us  [on_device(): lax.ppermute(ring[-1], 'term', [(dev, (dev + 1) % 8) for dev in range(8)])]
    ppermute x2, waiting for transfers between devices: 61.1 us -> 0.01 us  [extended(): lax.ppermute(lax.slice_in_dim(block, block.shape[dim] - width, None, axis...]
    psum x2, waiting for transfers between devices: 154 us -> 210 us  [on_device(): summed = lax.psum(total.reshape(full_count, sectors * width), 'term')]
    all_gather x2 -> x0, waiting for transfers between devices: 51.4 us -> none  [on_device(): full_rows = lax.all_gather(vector_bf, 'term', axis=1, tiled=True)]
    concatenate x0 -> x5, other arithmetic: none -> 12 us  [the longest x2 6.66 us: extended(): block = jnp.concatenate([low, block, high], axis=dim)]
  transfers between devices with their start and end apart: 8 -> 20, of which waited for: 8 -> 18; matrix products, arithmetic and copies ran while one was open for 1% -> 0% of each run, Pallas kernels for 0% -> 0%
where the time goes in v1:
time: 674 us; the launch traced here: 673 us
  waiting for transfers between devices  370 us (55%)
  blocking collectives  202 us (30%)
  matrix products  36.1 us (5%)
  other arithmetic  29.6 us (4%)
  between operations  20.3 us (3%)
  starting transfers between devices  13.7 us (2%)
    psum x2, waiting for transfers between devices, on_device(): summed = lax.psum(total.reshape(full_count, sectors * width), 'term')  210 us
    ppermute x14, waiting for transfers between devices, on_device(): lax.ppermute(ring[-1], 'term', [(dev, (dev + 1) % 8) for dev in range(8)])  97.1 us
    psum x2, blocking collectives, on_device(): alpha = lax.psum(jnp.sum(vector * image), ('sec', 'term'))  80.7 us
    psum x2, blocking collectives, on_device(): beta_square = lax.psum(jnp.sum(residual * residual), ('sec', 'term'))  79.1 us
    ppermute x2, waiting for transfers between devices, extended(): lax.ppermute(lax.slice_in_dim(block, 0, width, axis=dim), axis, backward)  63.1 us
    psum x1, blocking collectives, on_device(): norm_start = lax.psum(jnp.sum(start * start), ('sec', 'term'))  42.2 us
    dot_general x4, matrix products, on_device(): jnp.einsum('sij,sjk->isk', product, right_env[partial_term_index], prefer...  36.1 us
  transfers between devices with their start and end apart: 20, of which 18 were waited for; matrix products, arithmetic and copies ran while one was open for 0% of the time, Pallas kernels for 0%

profile of v1, /device:TPU:0, one launch (start us, length us, event | category | flops | bytes accessed | tf_op | source)
XLA Modules:
  0.0 672.9 jit_solution(10669873852891290281)
XLA Ops:
  10.2 42.2 %psum.49 = f32[]{:T(128)} all-reduce(f32[]{:T(128)} %multiply_reduce_fusion.2), channel_id=1, replica_groups=mesh['sec'=4,'term'=8] {'sec','term'}, use_global_device_ids=true, to_apply=%region_1.0 | all-reduce | flops 1 | bytes 8 | tf_op jit(solution)/shard_map/psum | solution.py:37
  54.3 6.9 %collective-permute-done = bf16[1,112,896]{2,1,0:T(8,128)(2,1)S(1)} collective-permute-done((bf16[1,112,896]{2,1,0:T(8,128)(2,1)S(1)}, bf16[1,112,896]{2,1,0:T(8,128)(2,1)S(1)}, u32[]{:S(2)}, u32[]{:S(2)}) %collective-permute-start) | collective-permute-done | bytes 200736 | tf_op jit(solution)/shard_map/ppermute | solution.py:47
  61.3 6.9 %collective-permute-done.1 = bf16[1,112,896]{2,1,0:T(8,128)(2,1)S(1)} collective-permute-done((bf16[1,112,896]{2,1,0:T(8,128)(2,1)S(1)}, bf16[1,112,896]{2,1,0:T(8,128)(2,1)S(1)}, u32[]{:S(2)}, u32[]{:S(2)}) %collective-permute-start.1) | collective-permute-done | bytes 200736 | tf_op jit(solution)/shard_map/ppermute | solution.py:47
  68.2 6.9 %collective-permute-done.2 = bf16[1,112,896]{2,1,0:T(8,128)(2,1)S(1)} collective-permute-done((bf16[1,112,896]{2,1,0:T(8,128)(2,1)S(1)}, bf16[1,112,896]{2,1,0:T(8,128)(2,1)S(1)}, u32[]{:S(2)}, u32[]{:S(2)}) %collective-permute-start.2) | collective-permute-done | bytes 200736 | tf_op jit(solution)/shard_map/ppermute | solution.py:47
  75.1 6.9 %collective-permute-done.3 = bf16[1,112,896]{2,1,0:T(8,128)(2,1)S(1)} collective-permute-done((bf16[1,112,896]{2,1,0:T(8,128)(2,1)S(1)}, bf16[1,112,896]{2,1,0:T(8,128)(2,1)S(1)}, u32[]{:S(2)}, u32[]{:S(2)}) %collective-permute-start.3) | collective-permute-done | bytes 200736 | tf_op jit(solution)/shard_map/ppermute | solution.py:47
  82.1 6.9 %collective-permute-done.4 = bf16[1,112,896]{2,1,0:T(8,128)(2,1)S(1)} collective-permute-done((bf16[1,112,896]{2,1,0:T(8,128)(2,1)S(1)}, bf16[1,112,896]{2,1,0:T(8,128)(2,1)S(1)}, u32[]{:S(2)}, u32[]{:S(2)}) %collective-permute-start.4) | collective-permute-done | bytes 200736 | tf_op jit(solution)/shard_map/ppermute | solution.py:47
  89.0 6.9 %collective-permute-done.5 = bf16[1,112,896]{2,1,0:T(8,128)(2,1)S(1)} collective-permute-done((bf16[1,112,896]{2,1,0:T(8,128)(2,1)S(1)}, bf16[1,112,896]{2,1,0:T(8,128)(2,1)S(1)}, u32[]{:S(2)}, u32[]{:S(2)}) %collective-permute-start.5) | collective-permute-done | bytes 200736 | tf_op jit(solution)/shard_map/ppermute | solution.py:47
  96.0 6.9 %collective-permute-done.6 = bf16[1,112,896]{2,1,0:T(8,128)(2,1)S(1)} collective-permute-done((bf16[1,112,896]{2,1,0:T(8,128)(2,1)S(1)}, bf16[1,112,896]{2,1,0:T(8,128)(2,1)S(1)}, u32[]{:S(2)}, u32[]{:S(2)}) %collective-permute-start.6) | collective-permute-done | bytes 200736 | tf_op jit(solution)/shard_map/ppermute | solution.py:47
  107.2 6.0 collective-permute-start.7
  117.0 29.1 %collective-permute-done.8 = bf16[1,896,896]{2,1,0:T(8,128)(2,1)S(1)} collective-permute-done((bf16[1,896,896]{2,1,0:T(8,128)(2,1)S(1)}, bf16[1,896,896]{2,1,0:T(8,128)(2,1)S(1)}, u32[]{:S(2)}, u32[]{:S(2)}) %collective-permute-start.8) | collective-permute-done | bytes 1605664 | tf_op jit(solution)/shard_map/ppermute | solution.py:18
  146.1 4.2 pad_maximum_fusion
  150.2 8.2 %fusion.15 = f32[896,896]{1,0:T(8,128)} fusion(bf16[2,1,896,896]{3,2,1,0:T(8,128)(2,1)} %param.11, bf16[3,896,896]{2,1,0:T(8,128)(2,1)} %pad_maximum_fusion, s32[]{:T(128)S(6)} %select_n.22, bf16[2,1,896,896]{3,2,1,0:T(8,128)(2,1)} %param.10), kind=kOutput, calls=%fused_computation.27 | convolution fusion | flops 2878095360 | bytes 8028164 | tf_op jit(solution)/shard_map/sij,sjk->isk/dot_general | solution.py:67
  158.5 10.1 %fusion.3 = f32[896,896]{1,0:T(8,128)} fusion(f32[896,896]{1,0:T(8,128)} %fusion.15, f32[896]{0:T(1024)S(1)} %fusion.52, f32[896]{0:T(1024)S(1)} %fusion.53, f32[]{:T(128)} %bitcast.8, f32[]{:T(128)} %bitcast, bf16[2,1,896,896]{3,2,1,0:T(8,128)(2,1)S(1)} %copy-done.2, bf16[3,896,896]{2,1,0:T(8,128)(2,1)} %pad_maximum_fusion, s32[]{:T(128)S(6)} %select_n.23, ...), kind=kOutput, calls=%fused_computation.11 | convolution fusion | flops 2882109440 | bytes 11248644 | tf_op jit(solution)/shard_map/sij,sjk->isk/dot_general | solution.py:67
  168.7 104.8 %all-reduce.3.cloned.1.call-done = f32[896,896]{1,0:T(8,128)} async-done(((f32[896,896]{1,0:T(8,128)}), f32[896,896]{1,0:T(8,128)}) %all-reduce.3.cloned.1.call-update) | async-done | bytes 3211280 | tf_op jit(solution)/shard_map/psum | solution.py:77
  275.2 40.4 %psum.51 = f32[]{:T(128)} all-reduce(f32[]{:T(128)} %fusion.50), channel_id=1, replica_groups=mesh['sec'=4,'term'=8] {'sec','term'}, use_global_device_ids=true, to_apply=%region_4.6 | all-reduce | flops 1 | bytes 8 | tf_op jit(solution)/shard_map/psum | solution.py:80
  318.0 39.6 %psum.52 = f32[]{:T(128)} all-reduce(f32[]{:T(128)} %multiply_reduce_fusion.1), channel_id=1, replica_groups=mesh['sec'=4,'term'=8] {'sec','term'}, use_global_device_ids=true, to_apply=%region_6.8 | all-reduce | flops 1 | bytes 8 | tf_op jit(solution)/shard_map/psum | solution.py:82
  360.1 6.9 %collective-permute-done.9 = bf16[1,112,896]{2,1,0:T(8,128)(2,1)S(1)} collective-permute-done((bf16[1,112,896]{2,1,0:T(8,128)(2,1)S(1)}, bf16[1,112,896]{2,1,0:T(8,128)(2,1)S(1)}, u32[]{:S(2)}, u32[]{:S(2)}) %collective-permute-start.9) | collective-permute-done | bytes 200736 | tf_op jit(solution)/shard_map/ppermute | solution.py:47
  367.0 6.9 %collective-permute-done.10 = bf16[1,112,896]{2,1,0:T(8,128)(2,1)S(1)} collective-permute-done((bf16[1,112,896]{2,1,0:T(8,128)(2,1)S(1)}, bf16[1,112,896]{2,1,0:T(8,128)(2,1)S(1)}, u32[]{:S(2)}, u32[]{:S(2)}) %collective-permute-start.10) | collective-permute-done | bytes 200736 | tf_op jit(solution)/shard_map/ppermute | solution.py:47
  374.0 6.9 %collective-permute-done.11 = bf16[1,112,896]{2,1,0:T(8,128)(2,1)S(1)} collective-permute-done((bf16[1,112,896]{2,1,0:T(8,128)(2,1)S(1)}, bf16[1,112,896]{2,1,0:T(8,128)(2,1)S(1)}, u32[]{:S(2)}, u32[]{:S(2)}) %collective-permute-start.11) | collective-permute-done | bytes 200736 | tf_op jit(solution)/shard_map/ppermute | solution.py:47
  380.9 6.9 %collective-permute-done.12 = bf16[1,112,896]{2,1,0:T(8,128)(2,1)S(1)} collective-permute-done((bf16[1,112,896]{2,1,0:T(8,128)(2,1)S(1)}, bf16[1,112,896]{2,1,0:T(8,128)(2,1)S(1)}, u32[]{:S(2)}, u32[]{:S(2)}) %collective-permute-start.12) | collective-permute-done | bytes 200736 | tf_op jit(solution)/shard_map/ppermute | solution.py:47
  387.9 6.9 %collective-permute-done.13 = bf16[1,112,896]{2,1,0:T(8,128)(2,1)S(1)} collective-permute-done((bf16[1,112,896]{2,1,0:T(8,128)(2,1)S(1)}, bf16[1,112,896]{2,1,0:T(8,128)(2,1)S(1)}, u32[]{:S(2)}, u32[]{:S(2)}) %collective-permute-start.13) | collective-permute-done | bytes 200736 | tf_op jit(solution)/shard_map/ppermute | solution.py:47
  394.8 6.9 %collective-permute-done.14 = bf16[1,112,896]{2,1,0:T(8,128)(2,1)S(1)} collective-permute-done((bf16[1,112,896]{2,1,0:T(8,128)(2,1)S(1)}, bf16[1,112,896]{2,1,0:T(8,128)(2,1)S(1)}, u32[]{:S(2)}, u32[]{:S(2)}) %collective-permute-start.14) | collective-permute-done | bytes 200736 | tf_op jit(solution)/shard_map/ppermute | solution.py:47
  401.7 6.9 %collective-permute-done.15 = bf16[1,112,896]{2,1,0:T(8,128)(2,1)S(1)} collective-permute-done((bf16[1,112,896]{2,1,0:T(8,128)(2,1)S(1)}, bf16[1,112,896]{2,1,0:T(8,128)(2,1)S(1)}, u32[]{:S(2)}, u32[]{:S(2)}) %collective-permute-start.15) | collective-permute-done | bytes 200736 | tf_op jit(solution)/shard_map/ppermute | solution.py:47
  408.9 2.6 fusion.4
  412.8 4.9 collective-permute-start.16
  417.7 34.0 %collective-permute-done.17 = bf16[1,896,896]{2,1,0:T(8,128)(2,1)S(1)} collective-permute-done((bf16[1,896,896]{2,1,0:T(8,128)(2,1)S(1)}, bf16[1,896,896]{2,1,0:T(8,128)(2,1)S(1)}, u32[]{:S(2)}, u32[]{:S(2)}) %collective-permute-start.17) | collective-permute-done | bytes 1605664 | tf_op jit(solution)/shard_map/ppermute | solution.py:18
  454.1 7.6 %fusion.13 = f32[896,896]{1,0:T(8,128)} fusion(bf16[2,1,896,896]{3,2,1,0:T(8,128)(2,1)S(1)} %copy-done.2, bf16[3,896,896]{2,1,0:T(8,128)(2,1)} %pad_maximum_fusion.1, s32[]{:T(128)S(6)} %select_n.22, bf16[2,1,896,896]{3,2,1,0:T(8,128)(2,1)} %param.10), kind=kOutput, calls=%fused_computation.25 | convolution fusion | flops 2878095360 | bytes 8028164 | tf_op jit(solution)/shard_map/sij,sjk->isk/dot_general | solution.py:67
  461.8 10.1 %fusion.1 = f32[896,896]{1,0:T(8,128)} fusion(f32[896,896]{1,0:T(8,128)} %fusion.13, f32[896]{0:T(1024)S(1)} %fusion.52, f32[896]{0:T(1024)S(1)} %fusion.53, f32[]{:T(128)} %bitcast.8, f32[]{:T(128)} %bitcast, bf16[2,1,896,896]{3,2,1,0:T(8,128)(2,1)S(1)} %copy-done.2, bf16[3,896,896]{2,1,0:T(8,128)(2,1)} %pad_maximum_fusion.1, s32[]{:T(128)S(6)} %select_n.23, ...), kind=kOutput, calls=%fused_computation.8 | convolution fusion | flops 2882109440 | bytes 11248644 | tf_op jit(solution)/shard_map/sij,sjk->isk/dot_general | solution.py:67
  471.9 104.7 %all-reduce.5.cloned.1.call-done = f32[896,896]{1,0:T(8,128)} async-done(((f32[896,896]{1,0:T(8,128)}), f32[896,896]{1,0:T(8,128)}) %all-reduce.5.cloned.1.call-update) | async-done | bytes 3211280 | tf_op jit(solution)/shard_map/psum | solution.py:77
  579.2 40.4 %psum.54 = f32[]{:T(128)} all-reduce(f32[]{:T(128)} %fusion.48), channel_id=1, replica_groups=mesh['sec'=4,'term'=8] {'sec','term'}, use_global_device_ids=true, to_apply=%region_9.11 | all-reduce | flops 1 | bytes 8 | tf_op jit(solution)/shard_map/psum | solution.py:80
  619.5 3.2 multiply_reduce_fusion
  622.7 39.5 %psum.55 = f32[]{:T(128)} all-reduce(f32[]{:T(128)} %get-tuple-element.4), channel_id=1, replica_groups=mesh['sec'=4,'term'=8] {'sec','term'}, use_global_device_ids=true, to_apply=%region_11.13 | all-reduce | flops 1 | bytes 8 | tf_op jit(solution)/shard_map/psum | solution.py:82
  (63 shorter events, 24.0 us)
Async XLA Ops:
  7.2 266.3 %all-reduce.3.cloned.1.call-start = ((), (), s32[]{:S(2)}) async-start(), calls=%async_computation | async-start | bytes 6422528 | tf_op jit(solution)/shard_map/psum | solution.py:77
  53.1 50.0 %copy-start = (bf16[1,112,896]{2,1,0:T(8,128)(2,1)S(1)}, bf16[1,112,896]{2,1,0:T(8,128)(2,1)}, u32[]{:S(2)}) copy-start(bf16[1,112,896]{2,1,0:T(8,128)(2,1)} %param.9) | copy-start | bytes 602116
  54.3 7.0 %collective-permute-start = (bf16[1,112,896]{2,1,0:T(8,128)(2,1)S(1)}, bf16[1,112,896]{2,1,0:T(8,128)(2,1)S(1)}, u32[]{:S(2)}, u32[]{:S(2)}) collective-permute-start(bf16[1,112,896]{2,1,0:T(8,128)(2,1)S(1)} %fusion.63), channel_id=1, source_target_pairs={{0,1},{1,2},{2,3},{3,4},{4,5},{5,6},{6,7},{7,0},{8,9},{9,10},{10,1... | collective-permute-start | bytes 602120 | tf_op jit(solution)/shard_map/ppermute | solution.py:47
  61.3 6.9 %collective-permute-start.1 = (bf16[1,112,896]{2,1,0:T(8,128)(2,1)S(1)}, bf16[1,112,896]{2,1,0:T(8,128)(2,1)S(1)}, u32[]{:S(2)}, u32[]{:S(2)}) collective-permute-start(bf16[1,112,896]{2,1,0:T(8,128)(2,1)S(1)} %collective-permute-done), channel_id=1, source_target_pairs={{0,1},{1,2},{2,3},{3,4},{4,5},{5,6},{6,7},{7,0},{8,9},{9,10},{10,1... | collective-permute-start | bytes 602120 | tf_op jit(solution)/shard_map/ppermute | solution.py:47
  68.2 6.9 %collective-permute-start.2 = (bf16[1,112,896]{2,1,0:T(8,128)(2,1)S(1)}, bf16[1,112,896]{2,1,0:T(8,128)(2,1)S(1)}, u32[]{:S(2)}, u32[]{:S(2)}) collective-permute-start(bf16[1,112,896]{2,1,0:T(8,128)(2,1)S(1)} %collective-permute-done.1), channel_id=1, source_target_pairs={{0,1},{1,2},{2,3},{3,4},{4,5},{5,6},{6,7},{7,0},{8,9},{9,10},{10,1... | collective-permute-start | bytes 602120 | tf_op jit(solution)/shard_map/ppermute | solution.py:47
  75.1 6.9 %collective-permute-start.3 = (bf16[1,112,896]{2,1,0:T(8,128)(2,1)S(1)}, bf16[1,112,896]{2,1,0:T(8,128)(2,1)S(1)}, u32[]{:S(2)}, u32[]{:S(2)}) collective-permute-start(bf16[1,112,896]{2,1,0:T(8,128)(2,1)S(1)} %collective-permute-done.2), channel_id=1, source_target_pairs={{0,1},{1,2},{2,3},{3,4},{4,5},{5,6},{6,7},{7,0},{8,9},{9,10},{10,1... | collective-permute-start | bytes 602120 | tf_op jit(solution)/shard_map/ppermute | solution.py:47
  82.1 6.9 %collective-permute-start.4 = (bf16[1,112,896]{2,1,0:T(8,128)(2,1)S(1)}, bf16[1,112,896]{2,1,0:T(8,128)(2,1)S(1)}, u32[]{:S(2)}, u32[]{:S(2)}) collective-permute-start(bf16[1,112,896]{2,1,0:T(8,128)(2,1)S(1)} %collective-permute-done.3), channel_id=1, source_target_pairs={{0,1},{1,2},{2,3},{3,4},{4,5},{5,6},{6,7},{7,0},{8,9},{9,10},{10,1... | collective-permute-start | bytes 602120 | tf_op jit(solution)/shard_map/ppermute | solution.py:47
  89.0 6.9 %collective-permute-start.5 = (bf16[1,112,896]{2,1,0:T(8,128)(2,1)S(1)}, bf16[1,112,896]{2,1,0:T(8,128)(2,1)S(1)}, u32[]{:S(2)}, u32[]{:S(2)}) collective-permute-start(bf16[1,112,896]{2,1,0:T(8,128)(2,1)S(1)} %collective-permute-done.4), channel_id=1, source_target_pairs={{0,1},{1,2},{2,3},{3,4},{4,5},{5,6},{6,7},{7,0},{8,9},{9,10},{10,1... | collective-permute-start | bytes 602120 | tf_op jit(solution)/shard_map/ppermute | solution.py:47
  96.0 6.9 %collective-permute-start.6 = (bf16[1,112,896]{2,1,0:T(8,128)(2,1)S(1)}, bf16[1,112,896]{2,1,0:T(8,128)(2,1)S(1)}, u32[]{:S(2)}, u32[]{:S(2)}) collective-permute-start(bf16[1,112,896]{2,1,0:T(8,128)(2,1)S(1)} %collective-permute-done.5), channel_id=1, source_target_pairs={{0,1},{1,2},{2,3},{3,4},{4,5},{5,6},{6,7},{7,0},{8,9},{9,10},{10,1... | collective-permute-start | bytes 602120 | tf_op jit(solution)/shard_map/ppermute | solution.py:47
  103.3 9.9 %copy-start.1 = (s32[2]{0:T(128)S(1)}, s32[2]{0:T(128)}, u32[]{:S(2)}) copy-start(s32[2]{0:T(128)} %param.12) | copy-start | bytes 28
  103.3 13.1 %copy-start.3 = (s32[2,1]{0,1:T(1,128)S(1)}, s32[2,1]{0,1:T(1,128)}, u32[]{:S(2)}) copy-start(s32[2,1]{0,1:T(1,128)} %param.13) | copy-start | bytes 28
  105.9 40.2 %collective-permute-start.8 = (bf16[1,896,896]{2,1,0:T(8,128)(2,1)S(1)}, bf16[1,896,896]{2,1,0:T(8,128)(2,1)S(1)}, u32[]{:S(2)}, u32[]{:S(2)}) collective-permute-start(bf16[1,896,896]{2,1,0:T(8,128)(2,1)S(1)} %fusion.5), channel_id=1, source_target_pairs={{8,0},{16,8},{24,16},{9,1},{17,9},{25,17},{10,2},{18,10},{26,18},{... | collective-permute-start | bytes 4816904 | tf_op jit(solution)/shard_map/ppermute | solution.py:18
  107.2 38.9 %collective-permute-start.7 = (bf16[1,896,896]{2,1,0:T(8,128)(2,1)S(1)}, bf16[1,896,896]{2,1,0:T(8,128)(2,1)}, u32[]{:S(2)}, u32[]{:S(2)}) collective-permute-start(bf16[1,896,896]{2,1,0:T(8,128)(2,1)S(1)} %fusion.5), channel_id=1, source_target_pairs={{0,8},{8,16},{16,24},{1,9},{9,17},{17,25},{2,10},{10,18},{18,26},{... | collective-permute-start | bytes 4816904 | tf_op jit(solution)/shard_map/ppermute | solution.py:15
  150.2 8.2 %copy-start.2 = (bf16[2,1,896,896]{3,2,1,0:T(8,128)(2,1)S(1)}, bf16[2,1,896,896]{3,2,1,0:T(8,128)(2,1)}, u32[]{:S(2)}) copy-start(bf16[2,1,896,896]{3,2,1,0:T(8,128)(2,1)} %param.11) | copy-start | bytes 9633796
  168.6 408.0 %all-reduce.5.cloned.1.call-start = ((), (), s32[]{:S(2)}) async-start(), calls=%async_computation.1 | async-start | bytes 6422528 | tf_op jit(solution)/shard_map/psum | solution.py:77
  360.1 7.0 %collective-permute-start.9 = (bf16[1,112,896]{2,1,0:T(8,128)(2,1)S(1)}, bf16[1,112,896]{2,1,0:T(8,128)(2,1)S(1)}, u32[]{:S(2)}, u32[]{:S(2)}) collective-permute-start(bf16[1,112,896]{2,1,0:T(8,128)(2,1)S(1)} %fusion.62), channel_id=1, source_target_pairs={{0,1},{1,2},{2,3},{3,4},{4,5},{5,6},{6,7},{7,0},{8,9},{9,10},{10,1... | collective-permute-start | bytes 602120 | tf_op jit(solution)/shard_map/ppermute | solution.py:47
  367.0 6.9 %collective-permute-start.10 = (bf16[1,112,896]{2,1,0:T(8,128)(2,1)S(1)}, bf16[1,112,896]{2,1,0:T(8,128)(2,1)S(1)}, u32[]{:S(2)}, u32[]{:S(2)}) collective-permute-start(bf16[1,112,896]{2,1,0:T(8,128)(2,1)S(1)} %collective-permute-done.9), channel_id=1, source_target_pairs={{0,1},{1,2},{2,3},{3,4},{4,5},{5,6},{6,7},{7,0},{8,9},{9,10},{10,1... | collective-permute-start | bytes 602120 | tf_op jit(solution)/shard_map/ppermute | solution.py:47
  374.0 6.9 %collective-permute-start.11 = (bf16[1,112,896]{2,1,0:T(8,128)(2,1)S(1)}, bf16[1,112,896]{2,1,0:T(8,128)(2,1)S(1)}, u32[]{:S(2)}, u32[]{:S(2)}) collective-permute-start(bf16[1,112,896]{2,1,0:T(8,128)(2,1)S(1)} %collective-permute-done.10), channel_id=1, source_target_pairs={{0,1},{1,2},{2,3},{3,4},{4,5},{5,6},{6,7},{7,0},{8,9},{9,10},{10,1... | collective-permute-start | bytes 602120 | tf_op jit(solution)/shard_map/ppermute | solution.py:47
  380.9 6.9 %collective-permute-start.12 = (bf16[1,112,896]{2,1,0:T(8,128)(2,1)S(1)}, bf16[1,112,896]{2,1,0:T(8,128)(2,1)S(1)}, u32[]{:S(2)}, u32[]{:S(2)}) collective-permute-start(bf16[1,112,896]{2,1,0:T(8,128)(2,1)S(1)} %collective-permute-done.11), channel_id=1, source_target_pairs={{0,1},{1,2},{2,3},{3,4},{4,5},{5,6},{6,7},{7,0},{8,9},{9,10},{10,1... | collective-permute-start | bytes 602120 | tf_op jit(solution)/shard_map/ppermute | solution.py:47
  387.9 6.9 %collective-permute-start.13 = (bf16[1,112,896]{2,1,0:T(8,128)(2,1)S(1)}, bf16[1,112,896]{2,1,0:T(8,128)(2,1)S(1)}, u32[]{:S(2)}, u32[]{:S(2)}) collective-permute-start(bf16[1,112,896]{2,1,0:T(8,128)(2,1)S(1)} %collective-permute-done.12), channel_id=1, source_target_pairs={{0,1},{1,2},{2,3},{3,4},{4,5},{5,6},{6,7},{7,0},{8,9},{9,10},{10,1... | collective-permute-start | bytes 602120 | tf_op jit(solution)/shard_map/ppermute | solution.py:47
  394.8 6.9 %collective-permute-start.14 = (bf16[1,112,896]{2,1,0:T(8,128)(2,1)S(1)}, bf16[1,112,896]{2,1,0:T(8,128)(2,1)S(1)}, u32[]{:S(2)}, u32[]{:S(2)}) collective-permute-start(bf16[1,112,896]{2,1,0:T(8,128)(2,1)S(1)} %collective-permute-done.13), channel_id=1, source_target_pairs={{0,1},{1,2},{2,3},{3,4},{4,5},{5,6},{6,7},{7,0},{8,9},{9,10},{10,1... | collective-permute-start | bytes 602120 | tf_op jit(solution)/shard_map/ppermute | solution.py:47
  401.7 6.9 %collective-permute-start.15 = (bf16[1,112,896]{2,1,0:T(8,128)(2,1)S(1)}, bf16[1,112,896]{2,1,0:T(8,128)(2,1)S(1)}, u32[]{:S(2)}, u32[]{:S(2)}) collective-permute-start(bf16[1,112,896]{2,1,0:T(8,128)(2,1)S(1)} %collective-permute-done.14), channel_id=1, source_target_pairs={{0,1},{1,2},{2,3},{3,4},{4,5},{5,6},{6,7},{7,0},{8,9},{9,10},{10,1... | collective-permute-start | bytes 602120 | tf_op jit(solution)/shard_map/ppermute | solution.py:47
  411.5 40.2 %collective-permute-start.17 = (bf16[1,896,896]{2,1,0:T(8,128)(2,1)S(1)}, bf16[1,896,896]{2,1,0:T(8,128)(2,1)S(1)}, u32[]{:S(2)}, u32[]{:S(2)}) collective-permute-start(bf16[1,896,896]{2,1,0:T(8,128)(2,1)S(1)} %fusion.4), channel_id=1, source_target_pairs={{8,0},{16,8},{24,16},{9,1},{17,9},{25,17},{10,2},{18,10},{26,18},{... | collective-permute-start | bytes 4816904 | tf_op jit(solution)/shard_map/ppermute | solution.py:18
  412.8 38.9 %collective-permute-start.16 = (bf16[1,896,896]{2,1,0:T(8,128)(2,1)S(1)}, bf16[1,896,896]{2,1,0:T(8,128)(2,1)S(1)}, u32[]{:S(2)}, u32[]{:S(2)}) collective-permute-start(bf16[1,896,896]{2,1,0:T(8,128)(2,1)S(1)} %fusion.4), channel_id=1, source_target_pairs={{0,8},{8,16},{16,24},{1,9},{9,17},{17,25},{2,10},{10,18},{18,26},{... | collective-permute-start | bytes 4816904 | tf_op jit(solution)/shard_map/ppermute | solution.py:15
Sparse Core Ops, SparseCore 0:
  168.7 104.6 all-reduce.2
  472.0 104.5 all-reduce.4
